TPU v7x, 512 devices: a whole 4x8x8 slice. The times are simulated.
512 devices in a mesh: sens: 4 (over z_lo), pts: 128 (over y, z_hi, x, core).
Axes of the slice: x: 4, y: 8, z: 8 (z_hi: 2, z_lo: 4; z = z_hi * 4 + z_lo), core: 2. Of those that a mesh axis runs over, the one named last changes fastest.
Arguments:
- params: float32 [24, 256, 2048], P('sens', 'pts'), may hold values from -6 to 6
- kernel: bfloat16 [2, 128, 2048, 257], P(None, 'sens', 'pts'), may hold values from -6 to 6
- coupled: int32 [128, 2048], P('sens', 'pts'), may hold values 0 or 1
- noise_prec: float32 [128, 256], P('sens'), may hold values from 4 to 32
- obs_len: int32 [128], P('sens'), may hold values from 128 to 256, as said below
Outputs:
- hessian_action: float32 [24, 256, 2048], P('sens', 'pts')
Inputs may be any that keep to these rules, and one draw needn't show every extreme that they name: A sensor's record is live for the time steps t < obs_len; some sensor records all 256 steps and some only 128.
All inputs are finite; a program needn't handle non-finite values. No bound on the sum of `coupled` on one device may be relied on, other than what follows from the above.
Results may differ from a plain program's by a relative error of at most 0.0037.
Values may be sent and summed in bfloat16 or wider, within the bound.
A program may use at most 64 MiB of HBM per device.

v0:
```python
import math

import jax
import jax.numpy as jnp
from jax import lax
from jax.sharding import PartitionSpec as P

GY = 32


highest = lax.Precision.HIGHEST
prior_delta = 0.5
prior_gamma = 1.0


def dft_tables(steps):
    length = 2 * steps
    times = jnp.arange(steps, dtype=jnp.int32)
    freqs = jnp.arange(steps + 1, dtype=jnp.int32)
    phase = times[:, None] * freqs[None, :] % length
    angle = phase.astype(jnp.float32) * (2.0 * math.pi / length)
    factor = 1.0 / math.sqrt(length)
    cosine = jnp.cos(angle) * factor
    sine = jnp.sin(angle) * factor
    doubled = jnp.where((freqs == 0) | (freqs == steps), 1.0, 2.0).astype(jnp.float32)
    return (cosine, -sine, (cosine * doubled[None, :]).T, (-sine * doubled[None, :]).T)


def cosine_table(count):
    modes = jnp.arange(count, dtype=jnp.int32)
    cells = jnp.arange(count, dtype=jnp.int32)
    phase = modes[:, None] * (2 * cells[None, :] + 1) % (4 * count)
    angle = phase.astype(jnp.float32) * (math.pi / (2 * count))
    norms = jnp.where(modes == 0, math.sqrt(1.0 / count), math.sqrt(2.0 / count)).astype(
        jnp.float32
    )
    return jnp.cos(angle) * norms[:, None]


def prior_symbol(rows, cols):
    eigen_rows = 2.0 - 2.0 * jnp.cos(
        jnp.arange(rows, dtype=jnp.int32).astype(jnp.float32) * (math.pi / rows)
    )
    eigen_cols = 2.0 - 2.0 * jnp.cos(
        jnp.arange(cols, dtype=jnp.int32).astype(jnp.float32) * (math.pi / cols)
    )
    return 1.0 / (prior_delta + prior_gamma * (eigen_rows[:, None] + eigen_cols[None, :]))


def prior_filter(field, rows, cols):
    grid = field.reshape(field.shape[:-1] + (rows, cols))
    table_rows = cosine_table(rows)
    table_cols = cosine_table(cols)
    coeffs = jnp.einsum("ai,...ij->...aj", table_rows, grid, precision=highest)
    coeffs = jnp.einsum("...aj,bj->...ab", coeffs, table_cols, precision=highest)
    coeffs = coeffs * prior_symbol(rows, cols)
    back = jnp.einsum("...ab,bj->...aj", coeffs, table_cols, precision=highest)
    back = jnp.einsum("ai,...aj->...ij", table_rows, back, precision=highest)
    return back.reshape(field.shape)


def transform(field, forward_cos, forward_sin):
    real_part = jnp.einsum("rtp,tf->prf", field, forward_cos, precision=highest)
    imag_part = jnp.einsum("rtp,tf->prf", field, forward_sin, precision=highest)
    return jnp.stack([real_part, imag_part]).astype(jnp.bfloat16)


def observe(freq_real, freq_imag, weight, tables):
    forward_cos, forward_sin, inverse_cos, inverse_sin = tables
    series = jnp.einsum("...f,ft->...t", freq_real, inverse_cos, precision=highest)
    series = series + jnp.einsum("...f,ft->...t", freq_imag, inverse_sin, precision=highest)
    series = series * weight
    real_part = jnp.einsum("...t,tf->...f", series, forward_cos, precision=highest)
    imag_part = jnp.einsum("...t,tf->...f", series, forward_sin, precision=highest)
    return jnp.stack([real_part, imag_part]).astype(jnp.bfloat16)


def on_device(params, kernel, coupled, noise_prec, obs_len):
    sens_rows = kernel.shape[1]
    nfreq = kernel.shape[3]
    steps = nfreq - 1
    total_points = params.shape[2]
    grid_rows = total_points // GY
    tables = dft_tables(steps)
    forward_cos, forward_sin, inverse_cos, inverse_sin = tables
    filtered = prior_filter(params, grid_rows, GY)
    points_field = lax.all_to_all(filtered, "pts", split_axis=2, concat_axis=1, tiled=True)
    gathered = lax.all_gather(points_field, "sens", axis=0, tiled=True)
    spectra = transform(gathered, forward_cos, forward_sin)
    masked = kernel * coupled[None, :, :, None].astype(jnp.bfloat16)
    with_real = jnp.einsum("spf,cprf->csrf", masked[0], spectra, preferred_element_type=jnp.float32)
    with_imag = jnp.einsum("spf,cprf->csrf", masked[1], spectra, preferred_element_type=jnp.float32)
    partials = jnp.stack([with_real[0] - with_imag[1], with_real[1] + with_imag[0]])
    scale_points = 1.0 / math.sqrt(total_points)
    live = (jnp.arange(steps, dtype=jnp.int32)[None, :] < obs_len[:, None]).astype(jnp.float32)
    weight_rows = noise_prec * live
    summed = lax.psum(partials, "pts") * scale_points
    residual = observe(summed[0], summed[1], weight_rows[:, None, :], tables)
    back_real = jnp.einsum(
        "spf,csrf->cprf", masked[0], residual, preferred_element_type=jnp.float32
    )
    back_imag = jnp.einsum(
        "spf,csrf->cprf", masked[1], residual, preferred_element_type=jnp.float32
    )
    adjoint_terms = jnp.stack([back_real[0] + back_imag[1], back_real[1] - back_imag[0]])
    total_sensors = sens_rows * lax.axis_size("sens")
    adjoint = lax.psum_scatter(adjoint_terms, "sens", scatter_dimension=2, tiled=True) * (
        1.0 / math.sqrt(total_sensors)
    )
    gradient = jnp.einsum("prf,ft->rtp", adjoint[0], inverse_cos, precision=highest)
    gradient = gradient + jnp.einsum("prf,ft->rtp", adjoint[1], inverse_sin, precision=highest)
    time_field = lax.all_to_all(gradient, "pts", split_axis=1, concat_axis=2, tiled=True)
    return prior_filter(time_field, grid_rows, GY)


def solution(mesh):
    placed = (
        P("sens", "pts", None),
        P(None, "sens", "pts", None),
        P("sens", "pts"),
        P("sens", None),
        P("sens"),
    )
    return jax.shard_map(
        on_device, mesh=mesh, in_specs=placed, out_specs=P("sens", "pts", None), check_vma=False
    )
```

profile of v0, /device:TPU:1, one launch (start us, length us, event | category | flops | bytes accessed | tf_op | source)
XLA Modules:
  0.0 1753.9 jit_solution(14356110899207540054)
XLA Ops:
  10.1 2.3 copy.115
  12.4 4.1 reshape.108
  16.5 21.0 %all-to-all-start = ((f32[128,1,192]{2,1,0:T(1,128)}), f32[128,1,192]{2,1,0:T(1,128)S(1)}, u32[]{:S(2)}, u32[]{:S(2)}) async-start(f32[128,1,192]{2,1,0:T(1,128)} %reshape.108), calls=%async_computation | async-start | bytes 262144 | tf_op jit(solution)/shard_map/all_to_all | solution.py:87
  37.6 3.5 copy.91
  41.1 1.7 broadcast_multiply_fusion.1
  42.8 10.7 all-to-all-done
  54.9 4.6 reshape.109
  59.5 4.7 copy.116
  64.1 1.7 copy.87
  66.1 13.2 all_gather.3
  79.3 1.9 fusion.4
  81.2 1.9 fusion.5
  83.2 3.2 copy.92
  86.4 3.0 convolution_bitcast_fusion
  90.6 2.9 slice_subtract_fusion
  93.5 4.6 copy.94
  98.1 3.3 copy.95
  101.4 3.2 pad_maximum_fusion.1
  105.4 1526.3 %all-reduce.2.cloned.1.call-done = f32[2,32,24,257]{3,2,1,0:T(8,128)} async-done(((f32[2,32,24,257]{3,2,1,0:T(8,128)}), f32[2,32,24,257]{3,2,1,0:T(8,128)}) %all-reduce.2.cloned.1.call-update) | async-done | bytes 1579024 | tf_op jit(solution)/shard_map/psum | solution.py:97
  1631.7 1.9 broadcast_multiply_fusion
  1633.6 2.4 fusion.3
  1636.0 2.4 fusion
  1638.4 2.4 fusion.1
  1640.8 2.4 fusion.2
  1644.5 5.9 copy.96
  1650.4 6.7 convolution_bitcast_fusion.3
  1657.1 5.3 convolution_bitcast_fusion.2
  1663.0 2.5 pad_maximum_fusion
  1665.5 4.7 copy.98
  1670.2 36.6 %reduce-scatter.2.cloned.1.call-done = f32[2,16,6,257]{3,1,0,2:T(8,128)} async-done(((f32[2,16,24,257]{3,1,0,2:T(8,128)}), f32[2,16,6,257]{3,1,0,2:T(8,128)}) %reduce-scatter.2.cloned.1.call-update) | async-done | bytes 197392 | tf_op jit(solution)/shard_map/reduce_scatter | solution.py:107
  1709.2 1.4 fusion.6
  1711.5 30.4 %all_to_all.33 = f32[128,1,192]{2,1,0:T(1,128)S(1)} all-to-all(f32[128,1,192]{2,1,0:T(1,128)S(1)} %reshape.110), channel_id=1, replica_groups=mesh['sens'=4,'pts'=128] {'pts'}, dimensions={0} | all-to-all | bytes 196608 | tf_op jit(solution)/shard_map/all_to_all | solution.py:112
  (56 shorter events, 17.4 us)
Async XLA Ops:
  10.0 27.5 %copy-start.3 = (bf16[2,32,16,257]{3,2,1,0:T(8,128)(2,1)S(1)}, bf16[2,32,16,257]{3,2,1,0:T(8,128)(2,1)}, u32[]{:S(2)}) copy-start(bf16[2,32,16,257]{3,2,1,0:T(8,128)(2,1)} %param.6) | copy-start | bytes 1579012
  16.5 24.5 %copy-start.5 = (s32[32,16]{0,1:T(8,128)S(1)}, s32[32,16]{0,1:T(8,128)}, u32[]{:S(2)}) copy-start(s32[32,16]{0,1:T(8,128)} %param.7) | copy-start | bytes 6148
  16.5 36.9 %all-to-all-start = ((f32[128,1,192]{2,1,0:T(1,128)}), f32[128,1,192]{2,1,0:T(1,128)S(1)}, u32[]{:S(2)}, u32[]{:S(2)}) async-start(f32[128,1,192]{2,1,0:T(1,128)} %reshape.108), calls=%async_computation | async-start | bytes 262144 | tf_op jit(solution)/shard_map/all_to_all | solution.py:87
  37.5 1594.2 %all-reduce.2.cloned.1.call-start = ((), (), s32[]{:S(2)}) async-start(), calls=%async_computation.3 | async-start | bytes 4718592 | tf_op jit(solution)/shard_map/psum | solution.py:97
  42.8 46.6 %copy-start = (bf16[2,32,16,257]{1,2,3,0:T(8,128)(2,1)}, bf16[2,32,16,257]{1,2,3,0:T(8,128)(2,1)S(1)}, u32[]{:S(2)}) copy-start(bf16[2,32,16,257]{1,2,3,0:T(8,128)(2,1)S(1)} %broadcast_multiply_fusion.1) | copy-start | bytes 1579012
  86.4 3.0 copy-start.2
  104.6 0.8 copy-start.4
  104.6 0.8 copy-start.6
  104.6 1602.3 %reduce-scatter.2.cloned.1.call-start = ((), (), s32[]{:S(2)}) async-start(), calls=%async_computation.4 | async-start | bytes 1474560 | tf_op jit(solution)/shard_map/reduce_scatter | solution.py:107
  1650.4 6.7 copy-start.1
Sparse Core Ops, SparseCore 0:
  104.7 1526.9 all-reduce.1
  1670.3 36.4 reduce-scatter.1
where the time goes:
time: 1760 us; the launch traced here: 1750 us
  waiting for transfers between devices  1570 us (89%)
  local copies, waits for them, and re-layouts  47.6 us (3%)
  blocking collectives  43.6 us (2%)
  matrix products  36.6 us (2%)
  starting transfers between devices  21.3 us (1%)
    psum x1, waiting for transfers between devices, on_device(): summed = lax.psum(partials, 'pts') * scale_points  1530 us
    reduce_scatter x1, waiting for transfers between devices, on_device(): lax.psum_scatter(adjoint_terms, 'sens', scatter_dimension=2, tiled=True)  36.6 us
  transfers between devices with their start and end apart: 3, of which 3 were waited for; matrix products, arithmetic and copies ran while one was open for 0% of the time, Pallas kernels for 0%

commit v1 on v0

v1 whole, which is shorter than its diff:
```python
import math

import jax
import jax.numpy as jnp
import numpy as np
from jax import lax
from jax.experimental import pallas as pl
from jax.experimental.pallas import tpu as pltpu
from jax.sharding import PartitionSpec as P

GY = 32
HALF = GY // 2
LANES = 128
SUB = 8
prior_delta = 0.5
prior_gamma = 1.0
f32 = jnp.float32
bf16 = jnp.bfloat16
PTS_SHAPE = (8, 2, 4, 2)


def cosine_table(count):
    k = np.arange(count)[:, None]
    i = np.arange(count)[None, :]
    norm = np.where(k == 0, math.sqrt(1.0 / count), math.sqrt(2.0 / count))
    return np.cos(math.pi * k * (2 * i + 1) / (2 * count)) * norm


def prior_symbol(rows, cols):
    er = 2.0 - 2.0 * np.cos(math.pi * np.arange(rows) / rows)
    ec = 2.0 - 2.0 * np.cos(math.pi * np.arange(cols) / cols)
    return 1.0 / (prior_delta + prior_gamma * (er[:, None] + ec[None, :]))


def packed_dft(steps):
    t = np.arange(steps)[:, None]
    f = np.arange(steps)[None, :]
    angle = 2.0 * math.pi * ((t * f) % (2 * steps)) / (2 * steps)
    real, imag = np.cos(angle), -np.sin(angle)
    imag[:, 0] = np.cos(math.pi * t[:, 0])
    return np.concatenate([real, imag], axis=1) / math.sqrt(2 * steps)


def split_table(table):
    high = table.astype(np.float32).astype(bf16)
    low = (table - high.astype(np.float64)).astype(np.float32).astype(bf16)
    return np.stack([high, low])


def make_tables(grid_rows, shape, own_rhs, steps, lane_pad):
    ny, nz, nx, nc = shape
    nxc = nx * nc
    npts = ny * nz * nxc
    cx, cy = cosine_table(grid_rows), cosine_table(GY)
    fields = 2 * own_rhs
    per = LANES // GY
    cols_in = np.kron(np.eye(per), cy.T)
    cols_out = np.kron(np.eye(per), cy)
    spread_rows = np.repeat(cx.T, 2, axis=0)
    out_half = np.zeros((2, fields * GY, 2 * lane_pad))
    in_half = np.zeros((2, 2, lane_pad, fields * GY))
    for h in range(2):
        part = cy[:, h * HALF : (h + 1) * HALF]
        for r in range(own_rhs):
            for e in range(2):
                field = (2 * r + e) * GY
                lane = r * HALF
                out_half[h, field : field + GY, e * lane_pad + lane : e * lane_pad + lane + HALF] = part
                in_half[h, e, lane : lane + HALF, field : field + GY] = part.T
    row = np.arange(npts)
    xc, rest = row // (nz * ny), row % (nz * ny)
    z, y = rest // ny, rest % ny
    owner = (y * nz + z) * nxc + xc
    gather_rows = np.zeros((2 * grid_rows, npts))
    for h in range(2):
        gather_rows[h * grid_rows : (h + 1) * grid_rows] = cx[:, owner // 2] * (owner % 2 == h)[None, :]
    dft = packed_dft(steps)
    dft_pairs = np.stack([dft[2 * owner], dft[2 * owner + 1]])
    small = dict(cols_in=cols_in, cols_out=cols_out, cx=cx, cxt=cx.T, spread_rows=spread_rows)
    small.update(out_half=out_half, gather_rows=gather_rows, in_half=in_half, dft=dft, dft_pairs=dft_pairs)
    tables = {name: split_table(table) for name, table in small.items()}
    tables["sigma"] = np.tile(prior_symbol(grid_rows, GY), (1, per)).astype(np.float32)
    return tables


TABLES = ("cols_in", "cols_out", "cx", "cxt", "spread_rows", "out_half")
TABLES += ("gather_rows", "in_half", "dft", "dft_pairs", "sigma")

RIGHT = ((1,), (0,))
BOTH_LAST = ((1,), (1,))
BOTH_FIRST = ((0,), (0,))


def dot(a, b, dims):
    return lax.dot_general(a, b, (dims, ((), ())), preferred_element_type=f32)


def halves(v):
    high = v.astype(bf16)
    return high, (v - high.astype(f32)).astype(bf16)


def dot_table(v, high, low, dims=RIGHT):
    vh, vl = halves(v)
    return dot(vh, high, dims) + (dot(vl, high, dims) + dot(vh, low, dims))


def same_row(ref, j, s, p):
    return jnp.broadcast_to(ref[j, s, pl.ds(p, 1), :], (SUB, ref.shape[-1]))


def table_dot(high, low, v):
    vh, vl = halves(v)
    return dot(high, vh, RIGHT) + (dot(high, vl, RIGHT) + dot(low, vh, RIGHT))


def kernel_body(cfg, *refs):
    (ny, nz, nx, nc), ns = cfg["shape"], cfg["sens"]
    nxc, nyz = nx * nc, ny * nz
    npts = nyz * nxc
    sensors, points, steps, own_rhs = cfg["sensors"], cfg["points"], cfg["steps"], cfg["own_rhs"]
    rhs = own_rhs * ns
    lane_pad = cfg["lane_pad"]
    grid_rows = cfg["grid_rows"]
    tiles = sensors * rhs // SUB
    rtiles = rhs // SUB
    xt = tiles // (nc * nx)
    owners = cfg["owners"]
    yt = xt // owners
    chunks = 2 * own_rhs * GY // LANES
    rows = own_rhs * points
    per = LANES // GY
    width = min(LANES, steps)

    field_ref, kernel_hbm, mask_ref, noise_ref, len_ref = refs[:5]
    ntab = len(TABLES)
    table_hbm = refs[5 : 5 + ntab]
    out_ref = refs[5 + ntab]
    scratch = list(refs[6 + ntab :])
    table_vmem = scratch[:ntab]
    (kraw, k1, k2, k3, k4, s1, r1, r2, s3, r3, sp, xf, x1, x2, x3, obs, d0, rc, d1, rx, d2, ry, d3, rz) = scratch[
        ntab : ntab + 24
    ]
    (resb, q1, q2, q3, adj, gs, gk, rg, t1, u1, u2, s4, u3, flat, load_sem, send_sem, recv_sem) = scratch[ntab + 24 :]
    tab = dict(zip(TABLES, table_vmem))

    my_s = lax.axis_index("sens")
    me = lax.axis_index("pts")
    my_y = me // (nz * nxc)
    my_z = (me // nxc) % nz
    my_xc = me % nxc
    my_x = my_xc // nc
    my_c = my_xc % nc

    def pts_at(y, z, xc):
        return (y * nz + z) * nxc + xc

    loads = [pltpu.make_async_copy(a, b, load_sem.at[i]) for i, (a, b) in enumerate(zip(table_hbm, table_vmem))]
    loads.append(pltpu.make_async_copy(kernel_hbm, kraw, load_sem.at[ntab]))
    for copy in loads:
        copy.start()

    partners = [(my_s, pts_at((my_y + d) % ny, my_z, my_xc)) for d in range(1, ny)]
    partners += [(my_s, pts_at(my_y, (my_z + d) % nz, my_xc)) for d in range(1, nz)]
    partners += [(my_s, pts_at(my_y, my_z, (my_xc + d) % nxc)) for d in range(1, nxc)]
    partners += [((my_s + d) % ns, me) for d in range(1, ns)]
    barrier = pltpu.get_barrier_semaphore()
    for target in partners:
        pl.semaphore_signal(barrier, inc=1, device_id=target, device_id_type=pl.DeviceIdType.MESH)

    used = [0]

    spans = [pl.ds(j * width, width) for j in range(steps // width)]

    def push(src, dst, target):
        i = used[0]
        used[0] += 1
        return pltpu.make_async_remote_copy(
            src_ref=src,
            dst_ref=dst,
            send_sem=send_sem.at[i],
            recv_sem=recv_sem.at[i],
            device_id=target,
            device_id_type=pl.DeviceIdType.MESH,
        )

    def run(copies):
        for copy in copies:
            copy.start()
        return copies

    def finish(copies):
        for copy in copies:
            copy.wait()

    near_y = sorted(range(ny), key=lambda d: min(d, ny - d))

    def relay(copies, came, left):
        onward = []
        for d in near_y:
            y = (my_y + ny - d) % ny
            if d:
                copies[d - 1].wait_recv()
            for e in range(1, nz):
                z = (my_z + e) % nz
                onward += run([push(came.at[y, z], left.at[my_z, y], (my_s, pts_at(my_y, z, my_xc)))])
        left[my_z] = came[:, my_z]
        for copy in copies:
            copy.wait_send()
        finish(onward)

    def modes_out(z):
        return z * tab["sigma"][...]

    for copy in loads[:ntab]:
        copy.wait()
    parity = lax.broadcasted_iota(jnp.int32, (npts, 2 * lane_pad), 0) % 2
    filtered = [jnp.zeros((npts, 2 * lane_pad), f32)] * 2
    for g in range(chunks):
        z = jnp.zeros((grid_rows, LANES), f32)
        for i in range(per):
            lines = pl.ds(i * GY, GY)
            z = z + dot_table(field_ref[g * per + i], tab["cols_in"][0, lines, :], tab["cols_in"][1, lines, :])
        z = modes_out(table_dot(tab["cx"][0], tab["cx"][1], z))
        z = table_dot(tab["spread_rows"][0], tab["spread_rows"][1], z)
        for h in range(2):
            span = pl.ds(g * LANES, LANES)
            filtered[h] = filtered[h] + dot_table(z, tab["out_half"][0, h, span, :], tab["out_half"][1, h, span, :])
    mixed = jnp.where(parity == 0, filtered[0], filtered[1])
    for e in range(2):
        s1[:, :, e] = mixed[:, e * lane_pad : (e + 1) * lane_pad].reshape(ny, nz, nxc, lane_pad)

    pl.semaphore_wait(barrier, len(partners))
    copies = run(
        [
            push(s1.at[(my_y + d) % ny], r1.at[my_y], (my_s, pts_at((my_y + d) % ny, my_z, my_xc)))
            for d in range(1, ny)
        ]
    )
    r1[my_y] = s1[my_y]

    loads[ntab].wait()
    first16 = lax.broadcasted_iota(jnp.int32, (points, steps), 1) == 0

    for s in range(sensors):
        keep = mask_ref[:, s : s + 1].astype(f32)
        real = kraw[0, s, :, :steps].astype(f32)
        imag = kraw[1, s, :, :steps].astype(f32)
        last = kraw[0, s, :, steps : steps + 1].astype(f32)
        imag = jnp.where(first16, 0.0, imag)
        plain = jnp.where(first16, last, real)
        for ref, value in ((k1, real + imag), (k2, plain), (k3, imag), (k4, real - imag)):
            for j, span in enumerate(spans):
                ref[j, s] = (value * keep)[:, j * width : (j + 1) * width]

    relay(copies, r1, r2)
    flat[...] = r2[...].reshape(nyz * 2 * nxc, lane_pad)
    for j in range(nxc):
        for e in range(2):
            s3[j, e] = flat[pl.ds(e * nxc + j, nyz, stride=2 * nxc), :]
    copies = run(
        [
            push(s3.at[(my_xc + d) % nxc], r3.at[my_xc], (my_s, pts_at(my_y, my_z, (my_xc + d) % nxc)))
            for d in range(1, nxc)
        ]
    )
    r3[my_xc] = s3[my_xc]
    finish(copies)

    spectra = jnp.zeros((lane_pad, 2 * steps), f32)
    for e in range(2):
        series = r3[:, e].reshape(npts, lane_pad)
        spectra = spectra + dot_table(series, tab["dft_pairs"][0, e], tab["dft_pairs"][1, e], BOTH_FIRST)
    sp[my_s] = spectra[:rows].astype(bf16)
    finish(run([push(sp.at[my_s], sp.at[my_s], ((my_s + d) % ns, me)) for d in range(1, ns)]))
    for k in range(ns):
        for q in range(2 * steps // width):
            xf[q, k * rows : (k + 1) * rows] = sp[k, :, q * width : (q + 1) * width].astype(f32)
    first_r = lax.broadcasted_iota(jnp.int32, (rhs, width), 1) == 0
    first_8 = lax.broadcasted_iota(jnp.int32, (SUB, width), 1) == 0
    for p in range(points):
        for j, span in enumerate(spans):
            c = xf[j, pl.ds(p, rhs, stride=points), :]
            d = xf[len(spans) + j, pl.ds(p, rhs, stride=points), :]
            x1[p, :, span] = c
            x2[p, :, span] = jnp.where(first_r, d, d - c) if j == 0 else d - c
            x3[p, :, span] = c + d

    def combine(real_terms, j, out, at):
        p1, p2, real = real_terms
        imag = p1 + p2
        if j == 0:
            out[at + (pl.ds(0, width),)] = jnp.where(first_8, real, real + real)
            out[at + (pl.ds(steps, width),)] = jnp.where(first_8, p2, imag + imag)
        else:
            out[at + (spans[j],)] = real + real
            out[at + (pl.ds(steps + j * width, width),)] = imag + imag

    def contract(i, carry):
        for j, span in enumerate(spans):
            acc = {}
            for p in range(points):
                for u in range(2):
                    ka, kb, kc = (same_row(k, j, 2 * i + u, p) for k in (k1, k2, k3))
                    for b in range(rtiles):
                        rr = pl.ds(b * SUB, SUB)
                        term = (ka * x1[p, rr, span], kb * x2[p, rr, span], kc * x3[p, rr, span])
                        old = acc.get((u, b))
                        acc[u, b] = term if old is None else tuple(o + t for o, t in zip(old, term))
            for (u, b), (p1, p2, p3) in acc.items():
                combine((p1, p2, p1 - p3), j, obs, (2 * i + u, pl.ds(b * SUB, SUB)))
        return carry

    block = xt // rtiles

    def predict(c, x):
        first = (c * nx + x) * block
        lax.fori_loop(first // 2, (first + block) // 2, contract, 0)
        value = obs[pl.ds(first, block)].reshape(block * rhs, 2 * steps)
        value = dot_table(value, tab["dft"][0], tab["dft"][1], BOTH_LAST)
        d0[c * nx + x] = value.reshape(xt, SUB, steps)

    other_c = (my_c + 1) % nc
    other = pts_at(my_y, my_z, my_x * nc + other_c)
    base_c, base_x = used[0], used[0] + nx
    used[0] += 2 * nx

    def place(i):
        return (my_x + i + 1) % nx

    def core_copy(i):
        x = place(i)
        return pltpu.make_async_remote_copy(
            src_ref=d0.at[other_c * nx + x],
            dst_ref=rc.at[x],
            send_sem=send_sem.at[base_c + i],
            recv_sem=recv_sem.at[base_c + i],
            device_id=(my_s, other),
            device_id_type=pl.DeviceIdType.MESH,
        )

    def x_copy(i):
        x = place(i)
        return pltpu.make_async_remote_copy(
            src_ref=d1.at[x],
            dst_ref=rx.at[i],
            send_sem=send_sem.at[base_x + i],
            recv_sem=recv_sem.at[base_x + i],
            device_id=(my_s, pts_at(my_y, my_z, x * nc + my_c)),
            device_id_type=pl.DeviceIdType.MESH,
        )

    def arrived(i):
        x = place(i)
        core_copy(i).wait_recv()
        d1[x] = d0[my_c * nx + x] + rc[x]

    def step(i, carry):
        predict(other_c, place(i))
        core_copy(i).start()
        predict(my_c, place(i))

        @pl.when(i > 0)
        def _():
            arrived(i - 1)
            x_copy(i - 1).start()

        return carry

    lax.fori_loop(0, nx, step, 0)
    arrived(nx - 1)
    total = d1[my_x]
    for i in range(nx - 1):
        x_copy(i).wait()
        total = total + rx[i]
    d2[...] = total
    for i in range(nx):
        core_copy(i).wait_send()

    owning = my_y < owners
    copies = [
        push(
            d2.at[pl.ds(lax.rem((my_y + d) % ny, owners) * yt, yt)],
            ry.at[d - 1],
            (my_s, pts_at((my_y + d) % ny, my_z, my_xc)),
        )
        for d in range(1, ny)
    ]
    for d, copy in zip(range(1, ny), copies):
        pl.when((my_y + d) % ny < owners)(copy.start)
    for d, copy in zip(range(1, ny), copies):
        pl.when((my_y + d) % ny < owners)(copy.wait_send)
        pl.when(owning)(copy.wait_recv)

    first_tile = (my_c * nx + my_x) * xt
    held = lax.rem(my_y, owners)
    y_tile = first_tile + held * yt
    z_copies = [push(d3, rz.at[my_z], (my_s, pts_at(my_y, (my_z + d) % nz, my_xc))) for d in range(1, nz)]

    @pl.when(owning)
    def _():
        total = d2[pl.ds(held * yt, yt)]
        for d in range(1, ny):
            total = total + ry[d - 1]
        d3[...] = total
        finish(run(z_copies))
        rz[my_z] = d3[...]
        total = rz[0]
        for z in range(1, nz):
            total = total + rz[z]
        for i in range(yt):
            s = (y_tile + i) // rtiles
            live = lax.broadcasted_iota(jnp.int32, (1, steps), 1) < len_ref[s]
            weight = jnp.where(live, noise_ref[pl.ds(s, 1), :], 0.0) * cfg["scale_points"]
            value = dot_table(total[i] * weight, tab["dft"][0], tab["dft"][1])
            resb[y_tile + i] = value.astype(bf16)

    def piece(c, x, y):
        return resb.at[pl.ds((c * nx + x) * xt + lax.rem(y, owners) * yt, yt)]

    mine = piece(my_c, my_x, my_y)
    y_copies = [push(mine, mine, (my_s, pts_at((my_y + d) % ny, my_z, my_xc))) for d in range(1, ny)]
    for copy in y_copies:
        pl.when(owning)(copy.start)
    x_copies, c_copies = {}, {}
    for d in near_y:
        y = (my_y + ny - d) % ny
        if d:
            pl.when(y < owners)(y_copies[d - 1].wait_recv)
        here = piece(my_c, my_x, y)
        x_copies[d] = [
            push(here, here, (my_s, pts_at(my_y, my_z, ((my_x + e) % nx) * nc + my_c))) for e in range(1, nx)
        ]
        sources = [piece(my_c, (my_x + nx - e) % nx, y) for e in range(nx)]
        c_copies[d] = [push(source, source, (my_s, other)) for source in sources]
        pl.when(y < owners)(lambda d=d: run(x_copies[d] + c_copies[d][:1]) and None)
    for d in near_y:
        y = (my_y + ny - d) % ny

        @pl.when(y < owners)
        def _(d=d):
            for e in range(1, nx):
                x_copies[d][e - 1].wait_recv()
                c_copies[d][e].start()

    for copy in y_copies:
        pl.when(owning)(copy.wait_send)
    for d in near_y:
        y = (my_y + ny - d) % ny

        @pl.when(y < owners)
        def _(d=d):
            for copy in x_copies[d]:
                copy.wait_send()
            finish(c_copies[d])

    def widen(s, carry):
        for b in range(rtiles):
            rr = pl.ds(b * SUB, SUB)
            for j, span in enumerate(spans):
                c = resb[s * rtiles + b, :, span].astype(f32)
                d = resb[s * rtiles + b, :, pl.ds(steps + j * width, width)].astype(f32)
                q1[s, rr, span] = c
                q2[s, rr, span] = jnp.where(first_8, d, d - c) if j == 0 else d - c
                q3[s, rr, span] = c + d
        return carry

    lax.fori_loop(0, sensors, widen, 0)

    def contract_back(i, carry):
        for j, span in enumerate(spans):
            acc = {}
            for s in range(sensors):
                for u in range(2):
                    ka, kb, kc = (same_row(k, j, s, 2 * i + u) for k in (k4, k2, k3))
                    for b in range(rtiles):
                        rr = pl.ds(b * SUB, SUB)
                        term = (ka * q1[s, rr, span], kb * q2[s, rr, span], kc * q3[s, rr, span])
                        old = acc.get((u, b))
                        acc[u, b] = term if old is None else tuple(o + t for o, t in zip(old, term))
            for (u, b), (p1, p2, p3) in acc.items():
                combine((p1, p2, p1 + p3), j, adj, (2 * i + u, pl.ds(b * SUB, SUB)))
        return carry

    lax.fori_loop(0, points // 2, contract_back, 0)

    value = dot_table(adj[...].reshape(points * rhs, 2 * steps), tab["dft"][0], tab["dft"][1], BOTH_LAST)
    for j in range(len(spans)):
        gs[j] = value[:, j * width : (j + 1) * width]
    for r in range(rhs):
        for j, span in enumerate(spans):
            gk[r // own_rhs, pl.ds((r % own_rhs) * points, points), span] = gs[
                j, pl.ds(r, points, stride=rhs), :
            ].astype(bf16)

    finish(run([push(gk.at[(my_s + d) % ns], rg.at[d - 1], ((my_s + d) % ns, me)) for d in range(1, ns)]))
    total = gk[my_s].astype(f32)
    for d in range(1, ns):
        total = total + rg[d - 1].astype(f32)
    total = total * cfg["scale_sensors"]
    if rows < lane_pad:
        total = jnp.concatenate([total, jnp.zeros((lane_pad - rows, steps), f32)], axis=0)
    t1[...] = jnp.transpose(total).reshape(ny, nz, 2 * nxc, lane_pad)

    copies = run(
        [
            push(t1.at[(my_y + d) % ny], u1.at[my_y], (my_s, pts_at((my_y + d) % ny, my_z, my_xc)))
            for d in range(1, ny)
        ]
    )
    u1[my_y] = t1[my_y]
    relay(copies, u1, u2)
    flat[...] = u2[...].reshape(nyz * 2 * nxc, lane_pad)
    for j in range(nxc):
        for e in range(2):
            s4[j, e] = flat[pl.ds(2 * j + e, nyz, stride=2 * nxc), :]
    copies = run(
        [
            push(s4.at[(my_xc + d) % nxc], u3.at[my_xc], (my_s, pts_at(my_y, my_z, (my_xc + d) % nxc)))
            for d in range(1, nxc)
        ]
    )
    u3[my_xc] = s4[my_xc]
    finish(copies)

    modes = jnp.zeros((grid_rows, chunks * LANES), f32)
    for e in range(2):
        field = u3[:, e].reshape(npts, lane_pad)
        field = table_dot(tab["gather_rows"][0], tab["gather_rows"][1], field)
        for h in range(2):
            part = field[h * grid_rows : (h + 1) * grid_rows]
            modes = modes + dot_table(part, tab["in_half"][0, h, e], tab["in_half"][1, h, e])
    for g in range(chunks):
        z = modes_out(modes[:, g * LANES : (g + 1) * LANES])
        z = table_dot(tab["cxt"][0], tab["cxt"][1], z)
        z = dot_table(z, tab["cols_out"][0], tab["cols_out"][1])
        for i in range(per):
            out_ref[g * per + i] = z[:, i * GY : (i + 1) * GY]


def on_device(shape, params, kernel, coupled, noise_prec, obs_len):
    ny, nz, nx, nc = shape
    ns = lax.axis_size("sens")
    npts = lax.axis_size("pts")
    own_rhs, own_steps, total_points = params.shape
    sensors, points, steps = kernel.shape[1], kernel.shape[2], kernel.shape[3] - 1
    grid_rows = total_points // GY
    rhs = own_rhs * ns
    lane_pad = LANES
    tiles = sensors * rhs // SUB
    xt = tiles // (nc * nx)
    owners = max(k for k in range(1, ny + 1) if xt % k == 0)
    yt = xt // owners
    rows = own_rhs * points
    fields = own_rhs * own_steps
    assert xt % (2 * (rhs // SUB)) == 0
    assert own_steps == 2 and points == HALF and npts == ny * nz * nx * nc and rows <= lane_pad
    cfg = dict(
        shape=shape,
        sens=ns,
        sensors=sensors,
        points=points,
        steps=steps,
        own_rhs=own_rhs,
        lane_pad=lane_pad,
        grid_rows=grid_rows,
        owners=owners,
        scale_points=1.0 / math.sqrt(total_points),
        scale_sensors=1.0 / math.sqrt(sensors * ns),
    )
    tables = make_tables(grid_rows, shape, own_rhs, steps, lane_pad)
    tables = [jnp.asarray(tables[name]) for name in TABLES]
    field = params.reshape(fields, grid_rows, GY)
    nxc, nyz = nx * nc, ny * nz
    vm = pltpu.VMEM
    scratch = [vm(t.shape, t.dtype) for t in tables]
    scratch += [vm(kernel.shape, kernel.dtype)]
    scratch += [vm((steps // min(LANES, steps), sensors, points, min(LANES, steps)), f32)] * 4
    scratch += [vm((ny, nz, 2, nxc, lane_pad), f32)] * 2
    scratch += [vm((nz, ny, 2, nxc, lane_pad), f32)]
    scratch += [vm((nxc, 2, nyz, lane_pad), f32)] * 2
    scratch += [vm((ns, rows, 2 * steps), bf16), vm((2 * steps // min(LANES, steps), ns * rows, min(LANES, steps)), f32)]
    scratch += [vm((points, rhs, steps), f32)] * 3
    scratch += [vm((sensors, rhs, 2 * steps), f32)]
    scratch += [vm((nc * nx, xt, SUB, steps), f32)] + [vm((nx, xt, SUB, steps), f32)] * 2
    scratch += [vm((max(nx - 1, 1), xt, SUB, steps), f32), vm((xt, SUB, steps), f32)]
    scratch += [vm((max(ny - 1, 1), yt, SUB, steps), f32), vm((yt, SUB, steps), f32)]
    scratch += [vm((nz, yt, SUB, steps), f32)]
    scratch += [vm((tiles, SUB, 2 * steps), bf16)]
    scratch += [vm((sensors, rhs, steps), f32)] * 3
    scratch += [vm((points, rhs, 2 * steps), f32), vm((steps // min(LANES, steps), points * rhs, min(LANES, steps)), f32)]
    scratch += [vm((ns, rows, steps), bf16), vm((max(ns - 1, 1), rows, steps), bf16)]
    scratch += [vm((ny, nz, 2 * nxc, lane_pad), f32)] * 2 + [vm((nz, ny, 2 * nxc, lane_pad), f32)]
    scratch += [vm((nxc, 2, nyz, lane_pad), f32)] * 2
    scratch += [vm((nyz * 2 * nxc, lane_pad), f32)]
    copies = 4 * ny + 2 * ny * nz + 2 * nxc + 2 * ns + 4 * nx + 2 * ny * nx + nz
    scratch += [
        pltpu.SemaphoreType.DMA((len(tables) + 1,)),
        pltpu.SemaphoreType.DMA((copies,)),
        pltpu.SemaphoreType.DMA((copies,)),
    ]
    whole = pl.BlockSpec(memory_space=pltpu.VMEM)
    scalars = pl.BlockSpec(memory_space=pltpu.SMEM)
    anywhere = pl.BlockSpec(memory_space=pl.ANY)
    out = pl.pallas_call(
        lambda *refs: kernel_body(cfg, *refs),
        out_shape=jax.ShapeDtypeStruct((fields, grid_rows, GY), f32),
        in_specs=[whole, anywhere, whole, whole, scalars] + [anywhere] * len(tables),
        out_specs=whole,
        scratch_shapes=scratch,
        compiler_params=pltpu.CompilerParams(
            collective_id=0, has_side_effects=True, vmem_limit_bytes=60 * 1024 * 1024
        ),
        name="hessian_action",
    )(field, kernel, coupled.T, noise_prec, obs_len, *tables)
    return out.reshape(params.shape)


def solution(mesh, shape=PTS_SHAPE):
    placed = (
        P("sens", "pts", None),
        P(None, "sens", "pts", None),
        P("sens", "pts"),
        P("sens", None),
        P("sens"),
    )
    return jax.shard_map(
        lambda *args: on_device(shape, *args),
        mesh=mesh,
        in_specs=placed,
        out_specs=P("sens", "pts", None),
        check_vma=False,
    )
```

time: 1760 us -> 110 us (0.06)
  waiting for transfers between devices: 1570 us -> 0 us
  Pallas kernels: 0 us -> 106 us
  local copies, waits for them, and re-layouts: 47.6 us -> 3.68 us
  blocking collectives: 43.6 us -> 0 us
  matrix products: 36.6 us -> 0 us
  starting transfers between devices: 21.3 us -> 0 us
    psum x1 -> x0, waiting for transfers between devices: 1530 us -> none  [on_device(): summed = lax.psum(partials, 'pts') * scale_points]
    pallas_call x0 -> x1, Pallas kernels: none -> 106 us  [on_device(): pl.pallas_call(lambda *refs: kernel_body(cfg, *refs), out_shape=jax.Shape...]
    dot_general x20 -> x0, matrix products: 36.6 us -> none  [the longest x1 6.7 us: on_device(): jnp.einsum('spf,csrf->cprf', masked[0], residual, preferred_element_type=...]
    reduce_scatter x1 -> x0, waiting for transfers between devices: 36.6 us -> none  [on_device(): lax.psum_scatter(adjoint_terms, 'sens', scatter_dimension=2, tiled=True)]
    all_to_all x1 -> x0, blocking collectives: 30.4 us -> none  [on_device(): lax.all_to_all(gradient, 'pts', split_axis=1, concat_axis=2, tiled=True)]
    all_to_all x1 -> x0, starting transfers between devices: 21 us -> none  [on_device(): lax.all_to_all(filtered, 'pts', split_axis=2, concat_axis=1, tiled=True)]
  transfers between devices with their start and end apart: 3 -> 0, of which waited for: 3 -> 0; matrix products, arithmetic and copies ran while one was open for 0% -> 0% of each run, Pallas kernels for 0% -> 0%
where the time goes in v1:
time: 110 us; the launch traced here: 109 us
  Pallas kernels  106 us (96%)
  local copies, waits for them, and re-layouts  3.68 us (3%)
    pallas_call x1, Pallas kernels, on_device(): pl.pallas_call(lambda *refs: kernel_body(cfg, *refs), out_shape=jax.Shape...  106 us

profile of v1, /device:TPU:1, one launch (start us, length us, event | category | flops | bytes accessed | tf_op | source)
XLA Modules:
  0.0 109.3 jit_solution(12093466964664037667)
XLA Ops:
  0.0 1.8 %reshape.6.refs_0_ = f32[12,64,32]{2,1,0:T(8,128)} reshape(f32[6,2,2048]{2,1,0:T(2,128)} %param.16) | data formatting | bytes 196608 | tf_op jit(solution)/shard_map/reshape | solution.py:573
  1.8 105.6 %hessian_action.1 = f32[12,64,32]{2,1,0:T(8,128)} custom-call(f32[12,64,32]{2,1,0:T(8,128)} %reshape.6.refs_0_, bf16[2,32,16,257]{3,2,1,0:T(8,128)(2,1)} %refs_1_.1, s32[16,32]{1,0:T(8,128)} %bitcast.1, f32[32,256]{1,0:T(8,128)} %refs_3_.1, s32[32]{0:T(128)} %refs_4_.1, bf16[2,128,128]{2,1,0:T(8,128)(2,1)} %constant.22.clone.refs_5_, ...), custom_call_target="tpu_custom_call" | custom-call | tf_op jit(solution)/shard_map/hessian_action/pallas_call | solution.py:605
  107.5 1.9 %reshape.7 = f32[6,2,2048]{2,1,0:T(2,128)} reshape(f32[12,64,32]{2,1,0:T(8,128)} %hessian_action.1) | data formatting | bytes 196608 | tf_op jit(solution)/shard_map/reshape | solution.py:616

commit v2 on v1

--- a/solution.py
+++ b/solution.py
@@ -83,8 +83,10 @@
     return tables
 
 
-TABLES = ("cols_in", "cols_out", "cx", "cxt", "spread_rows", "out_half")
-TABLES += ("gather_rows", "in_half", "dft", "dft_pairs", "sigma")
+TABLES = ("cols_in", "cx", "sigma", "spread_rows", "out_half")
+FIRST = len(TABLES)
+TABLES += ("dft_pairs", "dft", "gather_rows", "in_half")
+TABLES += ("cols_out", "cxt")
 
 RIGHT = ((1,), (0,))
 BOTH_LAST = ((1,), (1,))
@@ -212,7 +214,7 @@
     def modes_out(z):
         return z * tab["sigma"][...]
 
-    for copy in loads[:ntab]:
+    for copy in loads[:FIRST]:
         copy.wait()
     parity = lax.broadcasted_iota(jnp.int32, (npts, 2 * lane_pad), 0) % 2
     filtered = [jnp.zeros((npts, 2 * lane_pad), f32)] * 2
@@ -239,7 +241,8 @@
     )
     r1[my_y] = s1[my_y]
 
-    loads[ntab].wait()
+    for copy in loads[FIRST:]:
+        copy.wait()
     first16 = lax.broadcasted_iota(jnp.int32, (points, steps), 1) == 0
 
     for s in range(sensors):
@@ -482,25 +485,37 @@
                 combine((p1, p2, p1 + p3), j, adj, (2 * i + u, pl.ds(b * SUB, SUB)))
         return carry
 
-    lax.fori_loop(0, points // 2, contract_back, 0)
-
-    value = dot_table(adj[...].reshape(points * rhs, 2 * steps), tab["dft"][0], tab["dft"][1], BOTH_LAST)
-    for j in range(len(spans)):
-        gs[j] = value[:, j * width : (j + 1) * width]
-    for r in range(rhs):
-        for j, span in enumerate(spans):
-            gk[r // own_rhs, pl.ds((r % own_rhs) * points, points), span] = gs[
-                j, pl.ds(r, points, stride=rhs), :
-            ].astype(bf16)
-
-    finish(run([push(gk.at[(my_s + d) % ns], rg.at[d - 1], ((my_s + d) % ns, me)) for d in range(1, ns)]))
-    total = gk[my_s].astype(f32)
-    for d in range(1, ns):
-        total = total + rg[d - 1].astype(f32)
+    few = points // 2
+    sends = []
+    for h in range(2):
+        lax.fori_loop(h * few // 2, (h + 1) * few // 2, contract_back, 0)
+        value = adj[h * few : (h + 1) * few].reshape(few * rhs, 2 * steps)
+        value = dot_table(value, tab["dft"][0], tab["dft"][1], BOTH_LAST)
+        for j in range(len(spans)):
+            gs[j, h * few * rhs : (h + 1) * few * rhs] = value[:, j * width : (j + 1) * width]
+        for k in range(ns):
+            parts = []
+            for j in range(len(spans)):
+                lines = [
+                    gs[j, pl.ds(h * few * rhs + k * own_rhs + r, few, stride=rhs), :] for r in range(own_rhs)
+                ]
+                parts.append(jnp.concatenate(lines, axis=0))
+            gk[h, k] = jnp.concatenate(parts, axis=1).astype(bf16)
+        sends += run([push(gk.at[h, (my_s + d) % ns], rg.at[h, d - 1], ((my_s + d) % ns, me)) for d in range(1, ns)])
+    finish(sends)
+    sums = []
+    for h in range(2):
+        total = gk[h, my_s].astype(f32)
+        for d in range(1, ns):
+            total = total + rg[h, d - 1].astype(f32)
+        sums.append(total)
+    total = jnp.concatenate(
+        [sums[h][r * few : (r + 1) * few] for r in range(own_rhs) for h in range(2)], axis=0
+    )
     total = total * cfg["scale_sensors"]
     if rows < lane_pad:
         total = jnp.concatenate([total, jnp.zeros((lane_pad - rows, steps), f32)], axis=0)
-    t1[...] = jnp.transpose(total).reshape(ny, nz, 2 * nxc, lane_pad)
+    t1[...] = jnp.transpose(total).reshape(ny, nz, 2 * nxc, lane_pad).astype(bf16)
 
     copies = run(
         [
@@ -510,10 +525,10 @@
     )
     u1[my_y] = t1[my_y]
     relay(copies, u1, u2)
-    flat[...] = u2[...].reshape(nyz * 2 * nxc, lane_pad)
+    flat[...] = u2[...].astype(f32).reshape(nyz * 2 * nxc, lane_pad)
     for j in range(nxc):
         for e in range(2):
-            s4[j, e] = flat[pl.ds(2 * j + e, nyz, stride=2 * nxc), :]
+            s4[j, e] = flat[pl.ds(2 * j + e, nyz, stride=2 * nxc), :].astype(bf16)
     copies = run(
         [
             push(s4.at[(my_xc + d) % nxc], u3.at[my_xc], (my_s, pts_at(my_y, my_z, (my_xc + d) % nxc)))
@@ -526,7 +541,7 @@
     modes = jnp.zeros((grid_rows, chunks * LANES), f32)
     for e in range(2):
         field = u3[:, e].reshape(npts, lane_pad)
-        field = table_dot(tab["gather_rows"][0], tab["gather_rows"][1], field)
+        field = dot(tab["gather_rows"][0], field, RIGHT) + dot(tab["gather_rows"][1], field, RIGHT)
         for h in range(2):
             part = field[h * grid_rows : (h + 1) * grid_rows]
             modes = modes + dot_table(part, tab["in_half"][0, h, e], tab["in_half"][1, h, e])
@@ -589,11 +604,11 @@
     scratch += [vm((tiles, SUB, 2 * steps), bf16)]
     scratch += [vm((sensors, rhs, steps), f32)] * 3
     scratch += [vm((points, rhs, 2 * steps), f32), vm((steps // min(LANES, steps), points * rhs, min(LANES, steps)), f32)]
-    scratch += [vm((ns, rows, steps), bf16), vm((max(ns - 1, 1), rows, steps), bf16)]
-    scratch += [vm((ny, nz, 2 * nxc, lane_pad), f32)] * 2 + [vm((nz, ny, 2 * nxc, lane_pad), f32)]
-    scratch += [vm((nxc, 2, nyz, lane_pad), f32)] * 2
+    scratch += [vm((2, ns, rows // 2, steps), bf16), vm((2, max(ns - 1, 1), rows // 2, steps), bf16)]
+    scratch += [vm((ny, nz, 2 * nxc, lane_pad), bf16)] * 2 + [vm((nz, ny, 2 * nxc, lane_pad), bf16)]
+    scratch += [vm((nxc, 2, nyz, lane_pad), bf16)] * 2
     scratch += [vm((nyz * 2 * nxc, lane_pad), f32)]
-    copies = 4 * ny + 2 * ny * nz + 2 * nxc + 2 * ns + 4 * nx + 2 * ny * nx + nz
+    copies = 4 * ny + 2 * ny * nz + 2 * nxc + 3 * ns + 4 * nx + 2 * ny * nx + nz
     scratch += [
         pltpu.SemaphoreType.DMA((len(tables) + 1,)),
         pltpu.SemaphoreType.DMA((copies,)),

time: 110 us -> 107 us (0.973)
  Pallas kernels: 106 us -> 103 us
    pallas_call x1, Pallas kernels: 106 us -> 103 us  [on_device(): pl.pallas_call(lambda *refs: kernel_body(cfg, *refs), out_shape=jax.Shape...]
where the time goes in v2:
time: 107 us; the launch traced here: 106 us
  Pallas kernels  103 us (96%)
  local copies, waits for them, and re-layouts  3.68 us (3%)
    pallas_call x1, Pallas kernels, on_device(): pl.pallas_call(lambda *refs: kernel_body(cfg, *refs), out_shape=jax.Shape...  103 us

profile of v2, /device:TPU:1, one launch (start us, length us, event | category | flops | bytes accessed | tf_op | source)
XLA Modules:
  0.0 106.5 jit_solution(6787092328306408214)
XLA Ops:
  0.0 1.8 %reshape.6.refs_0_ = f32[12,64,32]{2,1,0:T(8,128)} reshape(f32[6,2,2048]{2,1,0:T(2,128)} %param.16) | data formatting | bytes 196608 | tf_op jit(solution)/shard_map/reshape | solution.py:588
  1.8 102.8 %hessian_action.1 = f32[12,64,32]{2,1,0:T(8,128)} custom-call(f32[12,64,32]{2,1,0:T(8,128)} %reshape.6.refs_0_, bf16[2,32,16,257]{3,2,1,0:T(8,128)(2,1)} %refs_1_.1, s32[16,32]{1,0:T(8,128)} %bitcast.1, f32[32,256]{1,0:T(8,128)} %refs_3_.1, s32[32]{0:T(128)} %refs_4_.1, bf16[2,128,128]{2,1,0:T(8,128)(2,1)} %constant.22.clone.refs_5_, ...), custom_call_target="tpu_custom_call" | custom-call | tf_op jit(solution)/shard_map/hessian_action/pallas_call | solution.py:620
  104.6 1.9 %reshape.7 = f32[6,2,2048]{2,1,0:T(2,128)} reshape(f32[12,64,32]{2,1,0:T(8,128)} %hessian_action.1) | data formatting | bytes 196608 | tf_op jit(solution)/shard_map/reshape | solution.py:631

commit v3 on v2

--- a/solution.py
+++ b/solution.py
@@ -1,3 +1,4 @@
+import functools
 import math
 
 import jax
@@ -274,21 +275,8 @@
     for e in range(2):
         series = r3[:, e].reshape(npts, lane_pad)
         spectra = spectra + dot_table(series, tab["dft_pairs"][0, e], tab["dft_pairs"][1, e], BOTH_FIRST)
-    sp[my_s] = spectra[:rows].astype(bf16)
-    finish(run([push(sp.at[my_s], sp.at[my_s], ((my_s + d) % ns, me)) for d in range(1, ns)]))
-    for k in range(ns):
-        for q in range(2 * steps // width):
-            xf[q, k * rows : (k + 1) * rows] = sp[k, :, q * width : (q + 1) * width].astype(f32)
     first_r = lax.broadcasted_iota(jnp.int32, (rhs, width), 1) == 0
     first_8 = lax.broadcasted_iota(jnp.int32, (SUB, width), 1) == 0
-    for p in range(points):
-        for j, span in enumerate(spans):
-            c = xf[j, pl.ds(p, rhs, stride=points), :]
-            d = xf[len(spans) + j, pl.ds(p, rhs, stride=points), :]
-            x1[p, :, span] = c
-            x2[p, :, span] = jnp.where(first_r, d, d - c) if j == 0 else d - c
-            x3[p, :, span] = c + d
-
     def combine(real_terms, j, out, at):
         p1, p2, real = real_terms
         imag = p1 + p2
@@ -299,26 +287,52 @@
             out[at + (spans[j],)] = real + real
             out[at + (pl.ds(steps + j * width, width),)] = imag + imag
 
-    def contract(i, carry):
-        for j, span in enumerate(spans):
-            acc = {}
-            for p in range(points):
-                for u in range(2):
-                    ka, kb, kc = (same_row(k, j, 2 * i + u, p) for k in (k1, k2, k3))
-                    for b in range(rtiles):
-                        rr = pl.ds(b * SUB, SUB)
-                        term = (ka * x1[p, rr, span], kb * x2[p, rr, span], kc * x3[p, rr, span])
-                        old = acc.get((u, b))
-                        acc[u, b] = term if old is None else tuple(o + t for o, t in zip(old, term))
-            for (u, b), (p1, p2, p3) in acc.items():
-                combine((p1, p2, p1 - p3), j, obs, (2 * i + u, pl.ds(b * SUB, SUB)))
+    def contract(j, i, carry):
+        span, acc = spans[j], {}
+        for p in range(points):
+            for u in range(2):
+                ka, kb, kc = (same_row(k, j, 2 * i + u, p) for k in (k1, k2, k3))
+                for b in range(rtiles):
+                    rr = pl.ds(b * SUB, SUB)
+                    term = (ka * x1[p, rr, span], kb * x2[p, rr, span], kc * x3[p, rr, span])
+                    old = acc.get((u, b))
+                    acc[u, b] = term if old is None else tuple(o + t for o, t in zip(old, term))
+        for (u, b), (p1, p2, p3) in acc.items():
+            combine((p1, p2, p1 - p3), j, obs, (2 * i + u, pl.ds(b * SUB, SUB)))
         return carry
+
+    parts = len(spans)
+    sends = []
+    for j in range(parts):
+        sp[j, my_s] = jnp.concatenate(
+            [
+                spectra[:rows, j * width : (j + 1) * width],
+                spectra[:rows, steps + j * width : steps + (j + 1) * width],
+            ],
+            axis=1,
+        ).astype(bf16)
+        sends.append(
+            run([push(sp.at[j, my_s], sp.at[j, my_s], ((my_s + d) % ns, me)) for d in range(1, ns)])
+        )
+    for j, span in enumerate(spans):
+        finish(sends[j])
+        for k in range(ns):
+            xf[j, k * rows : (k + 1) * rows] = sp[j, k, :, :width].astype(f32)
+            xf[parts + j, k * rows : (k + 1) * rows] = sp[j, k, :, width:].astype(f32)
+        for p in range(points):
+            c = xf[j, pl.ds(p, rhs, stride=points), :]
+            d = xf[parts + j, pl.ds(p, rhs, stride=points), :]
+            x1[p, :, span] = c
+            x2[p, :, span] = jnp.where(first_r, d, d - c) if j == 0 else d - c
+            x3[p, :, span] = c + d
+        if j < parts - 1:
+            lax.fori_loop(0, sensors // 2, functools.partial(contract, j), 0)
 
     block = xt // rtiles
 
     def predict(c, x):
         first = (c * nx + x) * block
-        lax.fori_loop(first // 2, (first + block) // 2, contract, 0)
+        lax.fori_loop(first // 2, (first + block) // 2, functools.partial(contract, parts - 1), 0)
         value = obs[pl.ds(first, block)].reshape(block * rhs, 2 * steps)
         value = dot_table(value, tab["dft"][0], tab["dft"][1], BOTH_LAST)
         d0[c * nx + x] = value.reshape(xt, SUB, steps)
@@ -494,13 +508,13 @@
         for j in range(len(spans)):
             gs[j, h * few * rhs : (h + 1) * few * rhs] = value[:, j * width : (j + 1) * width]
         for k in range(ns):
-            parts = []
+            pieces = []
             for j in range(len(spans)):
                 lines = [
                     gs[j, pl.ds(h * few * rhs + k * own_rhs + r, few, stride=rhs), :] for r in range(own_rhs)
                 ]
-                parts.append(jnp.concatenate(lines, axis=0))
-            gk[h, k] = jnp.concatenate(parts, axis=1).astype(bf16)
+                pieces.append(jnp.concatenate(lines, axis=0))
+            gk[h, k] = jnp.concatenate(pieces, axis=1).astype(bf16)
         sends += run([push(gk.at[h, (my_s + d) % ns], rg.at[h, d - 1], ((my_s + d) % ns, me)) for d in range(1, ns)])
     finish(sends)
     sums = []
@@ -594,7 +608,7 @@
     scratch += [vm((ny, nz, 2, nxc, lane_pad), f32)] * 2
     scratch += [vm((nz, ny, 2, nxc, lane_pad), f32)]
     scratch += [vm((nxc, 2, nyz, lane_pad), f32)] * 2
-    scratch += [vm((ns, rows, 2 * steps), bf16), vm((2 * steps // min(LANES, steps), ns * rows, min(LANES, steps)), f32)]
+    scratch += [vm((steps // min(LANES, steps), ns, rows, 2 * min(LANES, steps)), bf16), vm((2 * steps // min(LANES, steps), ns * rows, min(LANES, steps)), f32)]
     scratch += [vm((points, rhs, steps), f32)] * 3
     scratch += [vm((sensors, rhs, 2 * steps), f32)]
     scratch += [vm((nc * nx, xt, SUB, steps), f32)] + [vm((nx, xt, SUB, steps), f32)] * 2
@@ -608,7 +622,7 @@
     scratch += [vm((ny, nz, 2 * nxc, lane_pad), bf16)] * 2 + [vm((nz, ny, 2 * nxc, lane_pad), bf16)]
     scratch += [vm((nxc, 2, nyz, lane_pad), bf16)] * 2
     scratch += [vm((nyz * 2 * nxc, lane_pad), f32)]
-    copies = 4 * ny + 2 * ny * nz + 2 * nxc + 3 * ns + 4 * nx + 2 * ny * nx + nz
+    copies = 4 * ny + 2 * ny * nz + 2 * nxc + 4 * ns + 4 * nx + 2 * ny * nx + nz
     scratch += [
         pltpu.SemaphoreType.DMA((len(tables) + 1,)),
         pltpu.SemaphoreType.DMA((copies,)),

time: 107 us -> 106 us (level)
  no operation moved by 1% of the time
where the time goes in v3:
time: 106 us; the launch traced here: 105 us
  Pallas kernels  102 us (96%)
  local copies, waits for them, and re-layouts  3.68 us (3%)
    pallas_call x1, Pallas kernels, on_device(): pl.pallas_call(lambda *refs: kernel_body(cfg, *refs), out_shape=jax.Shape...  102 us

profile of v3, /device:TPU:1, one launch (start us, length us, event | category | flops | bytes accessed | tf_op | source)
XLA Modules:
  0.0 105.5 jit_solution(12020093251137356822)
XLA Ops:
  0.0 1.8 %reshape.6.refs_0_ = f32[12,64,32]{2,1,0:T(8,128)} reshape(f32[6,2,2048]{2,1,0:T(2,128)} %param.16) | data formatting | bytes 196608 | tf_op jit(solution)/shard_map/reshape | solution.py:602
  1.8 101.8 %hessian_action.1 = f32[12,64,32]{2,1,0:T(8,128)} custom-call(f32[12,64,32]{2,1,0:T(8,128)} %reshape.6.refs_0_, bf16[2,32,16,257]{3,2,1,0:T(8,128)(2,1)} %refs_1_.1, s32[16,32]{1,0:T(8,128)} %bitcast.1, f32[32,256]{1,0:T(8,128)} %refs_3_.1, s32[32]{0:T(128)} %refs_4_.1, bf16[2,128,128]{2,1,0:T(8,128)(2,1)} %constant.22.clone.refs_5_, ...), custom_call_target="tpu_custom_call" | custom-call | tf_op jit(solution)/shard_map/hessian_action/pallas_call | solution.py:634
  103.6 1.9 %reshape.7 = f32[6,2,2048]{2,1,0:T(2,128)} reshape(f32[12,64,32]{2,1,0:T(8,128)} %hessian_action.1) | data formatting | bytes 196608 | tf_op jit(solution)/shard_map/reshape | solution.py:645
